TPU v7x, 256 devices: a whole 4x4x8 slice. The times are simulated.
256 devices in a mesh: space: 16 (over x_hi, z), tm: 16 (over y, x_lo, core).
Axes of the slice: x: 4 (x_hi: 2, x_lo: 2; x = x_hi * 2 + x_lo), y: 4, z: 8, core: 2. Of those that a mesh axis runs over, the one named last changes fastest.
Arguments:
- snapshots: bfloat16 [163840, 8192], P('space', 'tm'), may hold values from -6 to 6
- modes: bfloat16 [163840, 256], P('space'), may hold values from -0.015625 to 0.015625
Outputs:
- gram: float32 [4864, 4864], P('tm', 'space')
- rhs: float32 [4864, 256], P('tm', 'space')
All inputs are finite; a program needn't handle non-finite values.
Results may differ from a plain program's by a relative error of at most 0.0057.
Values may be sent and summed in bfloat16 or wider, within the bound.
A program may use at most 128 MiB of HBM per device.

v0:
```python
import jax
import jax.numpy as jnp
from jax import lax
from jax.sharding import PartitionSpec as P

LEAD_MODES = 48
ridge_weight = 0.05


def passed_along(value, axis, steps):
    count = lax.axis_size(axis)
    leading, last = (max(0, -steps), min(count, count - steps))
    return lax.ppermute(value, axis, [(source, source + steps) for source in range(leading, last)])


def build_features(current, first, second):
    steps_count = current.shape[1]
    lead = first.shape[0]
    head = current[0:lead].astype(jnp.float32)
    prod_one = (head[:, None, :] * first.astype(jnp.float32)[None, :, :]).reshape(
        lead * lead, steps_count
    )
    prod_two = (head[:, None, :] * second.astype(jnp.float32)[None, :, :]).reshape(
        lead * lead, steps_count
    )
    return jnp.concatenate([current.astype(jnp.float32), prod_one, prod_two], axis=0).astype(
        jnp.bfloat16
    )


def neighbour(values, offset):
    return passed_along(values, "tm", offset)


def contract_rows(left, right):
    return lax.dot_general(
        left, right, (((1,), (1,)), ((), ())), preferred_element_type=jnp.float32
    )


def per_device(snapshots, modes):
    partial_sums = lax.dot_general(
        modes, snapshots, (((0,), (0,)), ((), ())), preferred_element_type=jnp.float32
    )
    coeffs = lax.psum(partial_sums, "space").astype(jnp.bfloat16)
    n_space = lax.axis_size("space")
    n_time = lax.axis_size("tm")
    modes_count = coeffs.shape[0]
    snap_local = coeffs.shape[1]
    total_snaps = snap_local * n_time
    lead = LEAD_MODES
    feature_count = modes_count + 2 * lead * lead
    col_block = feature_count // n_space
    target_block = modes_count // n_space
    row_block = feature_count // n_time
    space_pos = lax.axis_index("space")
    time_pos = lax.axis_index("tm")
    moved = {}
    for offset in (1, 2, -1):
        moved[offset] = neighbour(coeffs, offset)
    phi = build_features(coeffs, moved[1][0:lead], moved[2][0:lead])
    target = moved[-1]
    right = jnp.concatenate(
        [
            lax.dynamic_slice_in_dim(phi, space_pos * col_block, col_block, 0),
            lax.dynamic_slice_in_dim(target, space_pos * target_block, target_block, 0),
        ],
        axis=0,
    )
    joined = lax.psum_scatter(contract_rows(phi, right), "tm", scatter_dimension=0, tiled=True)
    row_global = time_pos * row_block + jnp.arange(row_block, dtype=jnp.int32)
    col_global = space_pos * col_block + jnp.arange(col_block, dtype=jnp.int32)
    diagonal_mask = (row_global[:, None] == col_global[None, :]).astype(jnp.float32)
    gram = joined[:, 0:col_block] / total_snaps + ridge_weight * diagonal_mask
    rhs = joined[:, col_block:] / total_snaps
    return (gram, rhs)


def solution(mesh):
    in_specs = (P("space", "tm"), P("space", None))
    out_specs = (P("tm", "space"), P("tm", "space"))
    return jax.shard_map(
        per_device, mesh=mesh, in_specs=in_specs, out_specs=out_specs, check_vma=False
    )
```

profile of v0, /device:TPU:4, one launch (start us, length us, event | category | flops | bytes accessed | tf_op | source)
XLA Modules:
  0.0 220.1 jit_solution(5401471481429606816)
XLA Ops:
  7.2 0.0 reduce-scatter.2.cloned.1.call-start
  7.2 7.2 %fusion.6 = f32[256,512]{1,0:T(8,128)S(1)} fusion(bf16[10240,256]{1,0:T(8,128)(2,1)} %param.3, bf16[10240,512]{1,0:T(8,128)(2,1)} %param.2), kind=kOutput, calls=%fused_computation.18 | convolution fusion | flops 2684354560 | bytes 16252928 | tf_op jit(solution)/shard_map/dot_general | solution.py:42
  14.4 83.4 %all-reduce.1 = bf16[256,512]{1,0:T(8,128)(2,1)S(1)} all-reduce(f32[256,512]{1,0:T(8,128)S(1)} %fusion.6), channel_id=1, replica_groups=mesh['space'=16,'tm'=16] {'space'}, use_global_device_ids=true, to_apply=%region_0.0 | all-reduce | flops 131072 | bytes 786432 | tf_op jit(solution)/shard_map/psum | solution.py:45
  97.9 4.0 %collective-permute-start.1 = (bf16[256,512]{1,0:T(8,128)(2,1)S(1)}, bf16[256,512]{1,0:T(8,128)(2,1)S(1)}, u32[]{:S(2)}, u32[]{:S(2)}) collective-permute-start(bf16[256,512]{1,0:T(8,128)(2,1)S(1)} %all-reduce.1), channel_id=1, source_target_pairs={{0,2},{1,3},{2,4},{3,5},{4,6},{5,7},{6,8},{7,9},{8,10},{9,11},{10,... | collective-permute-start | bytes 786440 | tf_op jit(solution)/shard_map/ppermute | solution.py:13
  101.9 1.3 collective-permute-start
  103.2 1.3 collective-permute-start.2
  104.6 1.8 collective-permute-done.1
  106.4 0.0 collective-permute-done
  106.4 1.5 multiply_convert_fusion.1
  107.9 0.4 pad_maximum_fusion
  108.3 0.0 collective-permute-done.2
  108.4 9.0 %fusion.1 = f32[4864,320]{1,0:T(8,128)} fusion(bf16[16,512]{1,0:T(8,128)(2,1)S(1)} %constant_dynamic-slice_fusion, bf16[304,512]{1,0:T(8,128)(2,1)S(1)} %constant_dynamic-slice_fusion.1, bf16[2304,512]{1,0:T(8,128)(2,1)S(1)} %bitcast.7, bf16[2304,512]{1,0:T(8,128)(2,1)S(1)} %bitcast.5, bf16[256,512]{1,0:T(8,128)(2,1)S(1)} %all-reduce.1), kind=kOutput, calls=%fused_computation.5 | convolution fusion | flops 1609433088 | bytes 11534336 | tf_op jit(solution)/shard_map/dot_general | solution.py:36
  117.3 0.0 reduce-scatter.2.cloned.1.call-update
  117.4 92.2 %reduce-scatter.2.cloned.1.call-done = f32[304,320]{1,0:T(8,128)} async-done(((f32[4864,320]{1,0:T(8,128)}), f32[304,320]{1,0:T(8,128)}) %reduce-scatter.2.cloned.1.call-update) | async-done | bytes 389136 | tf_op jit(solution)/shard_map/reduce_scatter | solution.py:70
  209.6 1.0 slice_multiply_fusion.1
  210.6 0.7 copy.4
  211.3 1.9 fusion
  (6 shorter events, 0.1 us)
Async XLA Ops:
  7.2 202.4 %reduce-scatter.2.cloned.1.call-start = ((), (), s32[]{:S(2)}) async-start(), calls=%async_computation.1 | async-start | bytes 7938048 | tf_op jit(solution)/shard_map/reduce_scatter | solution.py:70
  97.9 8.5 %collective-permute-start.1 = (bf16[256,512]{1,0:T(8,128)(2,1)S(1)}, bf16[256,512]{1,0:T(8,128)(2,1)S(1)}, u32[]{:S(2)}, u32[]{:S(2)}) collective-permute-start(bf16[256,512]{1,0:T(8,128)(2,1)S(1)} %all-reduce.1), channel_id=1, source_target_pairs={{0,2},{1,3},{2,4},{3,5},{4,6},{5,7},{6,8},{7,9},{8,10},{9,11},{10,... | collective-permute-start | bytes 786440 | tf_op jit(solution)/shard_map/ppermute | solution.py:13
  101.9 4.4 %collective-permute-start = (bf16[256,512]{1,0:T(8,128)(2,1)S(1)}, bf16[256,512]{1,0:T(8,128)(2,1)S(1)}, u32[]{:S(2)}, u32[]{:S(2)}) collective-permute-start(bf16[256,512]{1,0:T(8,128)(2,1)S(1)} %all-reduce.1), channel_id=1, source_target_pairs={{0,1},{1,2},{2,3},{3,4},{4,5},{5,6},{6,7},{7,8},{8,9},{9,10},{10,1... | collective-permute-start | bytes 786440 | tf_op jit(solution)/shard_map/ppermute | solution.py:13
  103.2 5.1 %collective-permute-start.2 = (bf16[256,512]{1,0:T(8,128)(2,1)S(1)}, bf16[256,512]{1,0:T(8,128)(2,1)S(1)}, u32[]{:S(2)}, u32[]{:S(2)}) collective-permute-start(bf16[256,512]{1,0:T(8,128)(2,1)S(1)} %all-reduce.1), channel_id=1, source_target_pairs={{1,0},{2,1},{3,2},{4,3},{5,4},{6,5},{7,6},{8,7},{9,8},{10,9},{11,1... | collective-permute-start | bytes 786440 | tf_op jit(solution)/shard_map/ppermute | solution.py:13
Sparse Core Ops, SparseCore 0:
  117.5 92.0 reduce-scatter.1
where the time goes:
time: 220 us
  waiting for transfers between devices  94 us (43%)
  blocking collectives  83.4 us (38%)
  matrix products  16.2 us (7%)
  between operations  14.2 us (6%)
  starting transfers between devices  6.68 us (3%)
  other arithmetic  4.85 us (2%)
    reduce_scatter x1, waiting for transfers between devices, per_device(): lax.psum_scatter(contract_rows(phi, right), 'tm', scatter_dimension=0, ti...  92.2 us
    psum x1, blocking collectives, per_device(): coeffs = lax.psum(partial_sums, 'space').astype(jnp.bfloat16)  83.4 us
    dot_general x1, matrix products, contract_rows(): lax.dot_general(left, right, (((1,), (1,)), ((), ())), preferred_element_...  8.97 us
    dot_general x1, matrix products, per_device(): lax.dot_general(modes, snapshots, (((0,), (0,)), ((), ())), preferred_ele...  7.22 us
    ppermute x3, starting transfers between devices, passed_along(): lax.ppermute(value, axis, [(source, source + steps) for source in range(l...  6.65 us
  transfers between devices with their start and end apart: 4, of which 2 were waited for; matrix products, arithmetic and copies ran while one was open for 1% of the time, Pallas kernels for 0%

commit v1 on v0

--- a/solution.py
+++ b/solution.py
@@ -2,9 +2,15 @@
 import jax.numpy as jnp
 from jax import lax
 from jax.sharding import PartitionSpec as P
+from jax.lax import all_gather
 
 LEAD_MODES = 48
 ridge_weight = 0.05
+
+
+def ends_raise(xs):
+    val2 = all_gather(xs, "space").sum(axis=0)
+    return val2
 
 
 def passed_along(value, axis, steps):
@@ -42,7 +48,7 @@
     partial_sums = lax.dot_general(
         modes, snapshots, (((0,), (0,)), ((), ())), preferred_element_type=jnp.float32
     )
-    coeffs = lax.psum(partial_sums, "space").astype(jnp.bfloat16)
+    coeffs = ends_raise(partial_sums).astype(jnp.bfloat16)
     n_space = lax.axis_size("space")
     n_time = lax.axis_size("tm")
     modes_count = coeffs.shape[0]

time: 220 us -> 282 us (1.28)
  waiting for transfers between devices: 94 us -> 233 us
  blocking collectives: 83.4 us -> 0 us
  other arithmetic: 4.85 us -> 9.21 us
    all_gather x0 -> x1, waiting for transfers between devices: none -> 136 us  [ends_raise(): val2 = all_gather(xs, 'space').sum(axis=0)]
    psum x1 -> x0, blocking collectives: 83.4 us -> none  [per_device(): coeffs = lax.psum(partial_sums, 'space').astype(jnp.bfloat16)]
    reduce_sum x0 -> x1, other arithmetic: none -> 4.36 us  [ends_raise(): val2 = all_gather(xs, 'space').sum(axis=0)]
  transfers between devices with their start and end apart: 4 -> 5, of which waited for: 2 -> 3; matrix products, arithmetic and copies ran while one was open for 1% -> 1% of each run, Pallas kernels for 0% -> 0%
where the time goes in v1:
time: 282 us
  waiting for transfers between devices  233 us (83%)
  matrix products  18.3 us (6%)
  between operations  14.2 us (5%)
  other arithmetic  9.21 us (3%)
  starting transfers between devices  6.67 us (2%)
    all_gather x1, waiting for transfers between devices, ends_raise(): val2 = all_gather(xs, 'space').sum(axis=0)  136 us
    reduce_scatter x1, waiting for transfers between devices, per_device(): lax.psum_scatter(contract_rows(phi, right), 'tm', scatter_dimension=0, ti...  93 us
    dot_general x1, matrix products, per_device(): lax.dot_general(modes, snapshots, (((0,), (0,)), ((), ())), preferred_ele...  9.27 us
    dot_general x1, matrix products, contract_rows(): lax.dot_general(left, right, (((1,), (1,)), ((), ())), preferred_element_...  9 us
    ppermute x3, starting transfers between devices, passed_along(): lax.ppermute(value, axis, [(source, source + steps) for source in range(l...  6.59 us
  transfers between devices with their start and end apart: 5, of which 3 were waited for; matrix products, arithmetic and copies ran while one was open for 1% of the time, Pallas kernels for 0%

profile of v1, /device:TPU:4, one launch (start us, length us, event | category | flops | bytes accessed | tf_op | source)
XLA Modules:
  0.0 281.6 jit_solution(13420012952386546855)
XLA Ops:
  7.2 0.0 all-gather.3.cloned.1.call-start
  7.2 9.3 %fusion.6 = f32[256,512]{1,0:T(8,128)} fusion(bf16[10240,256]{1,0:T(8,128)(2,1)} %param.3, bf16[10240,512]{1,0:T(8,128)(2,1)} %param.2), kind=kOutput, calls=%fused_computation.18 | convolution fusion | flops 2684354560 | bytes 16252928 | tf_op jit(solution)/shard_map/dot_general | solution.py:48
  16.5 0.0 all-gather.3.cloned.1.call-update
  16.5 0.0 reduce-scatter.2.cloned.1.call-start
  16.6 135.8 %all-gather.3.cloned.1.call-done = f32[4096,512]{1,0:T(8,128)} async-done(((f32[256,512]{1,0:T(8,128)}), f32[4096,512]{1,0:T(8,128)}) %all-gather.3.cloned.1.call-update) | async-done | bytes 8388624 | tf_op jit(solution)/shard_map/all_gather | solution.py:12
  152.3 4.4 %reduce_sum.9 = bf16[256,512]{1,0:T(8,128)(2,1)S(1)} reduce(f32[16,256,512]{2,1,0:T(8,128)} %bitcast.9, f32[]{:T(128)} %constant.10.clone.1), dimensions={0}, to_apply=%region_0.0 | reduce | flops 1966080 | bytes 8650756 | tf_op jit(solution)/shard_map/reduce_sum | solution.py:12
  156.7 4.0 %collective-permute-start.1 = (bf16[256,512]{1,0:T(8,128)(2,1)S(1)}, bf16[256,512]{1,0:T(8,128)(2,1)S(1)}, u32[]{:S(2)}, u32[]{:S(2)}) collective-permute-start(bf16[256,512]{1,0:T(8,128)(2,1)S(1)} %reduce_sum.9), channel_id=1, source_target_pairs={{0,2},{1,3},{2,4},{3,5},{4,6},{5,7},{6,8},{7,9},{8,10},{9,11},{10,... | collective-permute-start | bytes 786440 | tf_op jit(solution)/shard_map/ppermute | solution.py:19
  160.7 1.3 collective-permute-start
  162.0 1.3 collective-permute-start.2
  163.3 3.7 %collective-permute-done.1 = bf16[256,512]{1,0:T(8,128)(2,1)S(1)} collective-permute-done((bf16[256,512]{1,0:T(8,128)(2,1)S(1)}, bf16[256,512]{1,0:T(8,128)(2,1)S(1)}, u32[]{:S(2)}, u32[]{:S(2)}) %collective-permute-start.1) | collective-permute-done | bytes 262176 | tf_op jit(solution)/shard_map/ppermute | solution.py:19
  167.0 0.0 collective-permute-done
  167.1 1.5 multiply_convert_fusion.1
  168.6 0.4 pad_maximum_fusion
  169.0 0.0 collective-permute-done.2
  169.0 9.0 %fusion.1 = f32[4864,320]{1,0:T(8,128)} fusion(bf16[16,512]{1,0:T(8,128)(2,1)S(1)} %constant_dynamic-slice_fusion, bf16[304,512]{1,0:T(8,128)(2,1)S(1)} %constant_dynamic-slice_fusion.1, bf16[2304,512]{1,0:T(8,128)(2,1)S(1)} %bitcast.8, bf16[2304,512]{1,0:T(8,128)(2,1)S(1)} %bitcast.6, bf16[256,512]{1,0:T(8,128)(2,1)S(1)} %reduce_sum.9), kind=kOutput, calls=%fused_computation.5 | convolution fusion | flops 1609433088 | bytes 11534336 | tf_op jit(solution)/shard_map/dot_general | solution.py:42
  178.0 0.0 reduce-scatter.2.cloned.1.call-update
  178.1 93.0 %reduce-scatter.2.cloned.1.call-done = f32[304,320]{1,0:T(8,128)} async-done(((f32[4864,320]{1,0:T(8,128)}), f32[304,320]{1,0:T(8,128)}) %reduce-scatter.2.cloned.1.call-update) | async-done | bytes 389136 | tf_op jit(solution)/shard_map/reduce_scatter | solution.py:76
  271.1 1.0 slice_multiply_fusion.1
  272.1 0.7 copy.4
  272.8 1.9 fusion
  (6 shorter events, 0.1 us)
Async XLA Ops:
  7.2 145.1 %all-gather.3.cloned.1.call-start = ((), (), s32[]{:S(2)}) async-start(), calls=%async_computation.2 | async-start | bytes 8912896 | tf_op jit(solution)/shard_map/all_gather | solution.py:12
  16.5 254.6 %reduce-scatter.2.cloned.1.call-start = ((), (), s32[]{:S(2)}) async-start(), calls=%async_computation.1 | async-start | bytes 7938048 | tf_op jit(solution)/shard_map/reduce_scatter | solution.py:76
  156.7 10.3 %collective-permute-start.1 = (bf16[256,512]{1,0:T(8,128)(2,1)S(1)}, bf16[256,512]{1,0:T(8,128)(2,1)S(1)}, u32[]{:S(2)}, u32[]{:S(2)}) collective-permute-start(bf16[256,512]{1,0:T(8,128)(2,1)S(1)} %reduce_sum.9), channel_id=1, source_target_pairs={{0,2},{1,3},{2,4},{3,5},{4,6},{5,7},{6,8},{7,9},{8,10},{9,11},{10,... | collective-permute-start | bytes 786440 | tf_op jit(solution)/shard_map/ppermute | solution.py:19
  160.7 6.4 %collective-permute-start = (bf16[256,512]{1,0:T(8,128)(2,1)S(1)}, bf16[256,512]{1,0:T(8,128)(2,1)S(1)}, u32[]{:S(2)}, u32[]{:S(2)}) collective-permute-start(bf16[256,512]{1,0:T(8,128)(2,1)S(1)} %reduce_sum.9), channel_id=1, source_target_pairs={{0,1},{1,2},{2,3},{3,4},{4,5},{5,6},{6,7},{7,8},{8,9},{9,10},{10,1... | collective-permute-start | bytes 786440 | tf_op jit(solution)/shard_map/ppermute | solution.py:19
  162.0 7.0 %collective-permute-start.2 = (bf16[256,512]{1,0:T(8,128)(2,1)S(1)}, bf16[256,512]{1,0:T(8,128)(2,1)S(1)}, u32[]{:S(2)}, u32[]{:S(2)}) collective-permute-start(bf16[256,512]{1,0:T(8,128)(2,1)S(1)} %reduce_sum.9), channel_id=1, source_target_pairs={{1,0},{2,1},{3,2},{4,3},{5,4},{6,5},{7,6},{8,7},{9,8},{10,9},{11,1... | collective-permute-start | bytes 786440 | tf_op jit(solution)/shard_map/ppermute | solution.py:19
Sparse Core Ops, SparseCore 0:
  16.6 135.6 all-gather.2
  178.2 92.8 reduce-scatter.1
